TPU v7x, 32 devices: a whole 2x2x4 slice. The times are simulated.
32 devices in a mesh: blk: 8 (over z, y), pair: 4 (over x, core).
Axes of the slice: x: 2, y: 2, z: 4, core: 2. Of those that a mesh axis runs over, the one named last changes fastest.
Arguments:
- amplitudes: bfloat16 [64, 262144], P('pair', 'blk'), may hold values from -6 to 6
- integrals: bfloat16 [5120, 4, 128, 128], P(('blk', 'pair')), may hold values from -0.25 to 0.25
- block_irrep: int32 [2048], replicated, may hold values from 0 to 7
- slab_blocks: int32 [32], replicated, may hold values from 0 to 2047, as said below
- owner: int32 [2048], replicated, may hold values from 0 to 31, as said below
- partner: int32 [2048], replicated, may hold values from 0 to 2047, as said below
- sign: int32 [2048], replicated, may hold values from -1 to 1, as said below
Outputs:
- ladder: bfloat16 [64, 262144], P('pair', 'blk')
Inputs may be any that keep to these rules, and one draw needn't show every extreme that they name: Distinct blocks; block_irrep[slab_blocks[g * 4 + k]] = g. `owner`: flat device index (blk index times the pair axis's size plus pair index). For each blk index t, of the blocks t * 256 to t * 256 + 255 exactly 256 divided by the pair axis's size are stored on each pair index, at most 20 on any one device, and some device stores exactly 20 of them for every t. Integral rows not named by any block are read by no output. An involution without fixed points; for any blk indices t and t2, equal or not, exactly 256 divided by the blk axis's size of the blocks of t have their partner among the blocks of t2. `sign`: each entry is -1 or 1.
All inputs are finite; a program needn't handle non-finite values.
Results may differ from a plain program's by a relative error of at most 0.001.
Values may be sent and summed in bfloat16 or wider, within the bound.
A program may use at most 128 MiB of HBM per device.

v0:
```python
import functools

import jax
import jax.numpy as jnp
from jax import lax
from jax.experimental import pallas as pl
from jax.experimental.pallas import tpu as pltpu
from jax.sharding import PartitionSpec as P

TOP = 32766.0
STEPS = 256.0
TINY = 2.0**-120
MESH = pl.DeviceIdType.MESH


def prep_kernel(
    sizes,
    slab_ref,
    owner_ref,
    partner_ref,
    irrep_ref,
    sign_ref,
    amp_hbm,
    irrep_out,
    meta_out,
    picked,
    raw,
    pick_sem,
):
    blks, pairs, span, cap, per_irrep, slab_count, rows, width = sizes
    me_blk = lax.axis_index("blk")
    me = me_blk * pairs + lax.axis_index("pair")

    def pick(n):
        at = jnp.clip(slab_ref[n] - me_blk * span, 0, span - 1) * width
        return pltpu.make_async_copy(
            amp_hbm.at[:, pl.ds(pl.multiple_of(at, width), width)], raw.at[n], pick_sem.at[n]
        )

    for n in range(slab_count):
        pick(n).start()

    down = lax.broadcasted_iota(jnp.int32, (span, span), 0)
    across = lax.broadcasted_iota(jnp.int32, (span, span), 1)
    diagonal = down == across
    earlier = down < across

    def column(row):
        return jnp.sum(jnp.where(diagonal, row, 0.0), axis=1, keepdims=True)

    def count(mask):
        return jnp.sum(jnp.where(mask, 1.0, 0.0), axis=0, keepdims=True)

    def placed(keys, values):
        hit = keys == across.astype(jnp.float32)
        return jnp.sum(jnp.where(hit, values, 0.0), axis=0, keepdims=True)

    parts = span // width

    def mine(ref):
        found = [ref[pl.ds(me_blk * parts + part, 1), :] for part in range(parts)]
        return jnp.concatenate(found, axis=1).astype(jnp.float32)

    def every(ref):
        found = [ref[pl.ds(part, blks, stride=parts), :] for part in range(parts)]
        return jnp.concatenate(found, axis=1)

    owner, partner, sign = mine(owner_ref), mine(partner_ref), mine(sign_ref)
    partner_blk = jnp.floor((partner + 0.5) * (1.0 / span))
    owner_col, partner_col, blk_col = column(owner), column(partner), column(partner_blk)
    same_blk = blk_col == partner_blk
    rank = count(jnp.logical_and(owner_col == owner, earlier))
    send_key = partner_blk * (span // blks) + count(jnp.logical_and(same_blk, earlier))
    mirror_rank = count(jnp.logical_and(same_blk, partner_col < partner))
    key_col = column(send_key)
    send_dev = placed(key_col, owner_col)
    send_rank = placed(key_col, column(rank))
    for at, row in enumerate((owner, rank, send_dev, send_rank, partner_blk, mirror_rank, sign)):
        meta_out[at : at + 1, :] = row.astype(jnp.int32)

    stored = every(owner_ref) == me
    ranks = jnp.dot(
        jnp.where(stored, 1.0, 0.0).astype(jnp.bfloat16),
        jnp.where(earlier, 1.0, 0.0).astype(jnp.bfloat16),
        preferred_element_type=jnp.float32,
    ).astype(jnp.int32)
    ranks = jnp.where(stored, ranks, -1)
    irrep = every(irrep_ref).astype(jnp.float32)
    lane = lax.broadcasted_iota(jnp.int32, (blks, width), 1)
    slots = jnp.zeros((blks, width), jnp.float32)
    for r in range(cap):
        found = jnp.sum(jnp.where(ranks == r, irrep, 0.0), axis=1, keepdims=True)
        slots = jnp.where(lane == r, found, slots)
    irrep_out[...] = slots.astype(jnp.int32)

    for n in range(slab_count):
        pick(n).wait()
    for n in range(slab_count):
        local = slab_ref[n] - me_blk * span
        inside = jnp.logical_and(local >= 0, local < span).astype(jnp.float32)
        picked[n] = (raw[n].astype(jnp.float32) * inside).astype(jnp.bfloat16)


def kernel(
    sizes,
    irrep_ref,
    meta_ref,
    picked,
    ints_hbm,
    out_ref,
    ints,
    picked_in,
    slab_in,
    slab,
    send1,
    recv1,
    own,
    send2,
    recv2,
    facing,
    ints_sem,
    pick_send,
    pick_recv,
    gath_send,
    gath_recv,
    fwd_send,
    fwd_recv,
    send1_sem,
    recv1_sem,
    send2_sem,
    recv2_sem,
):
    blks, pairs, span, cap, per_irrep, slab_count, rows, width = sizes
    devices = blks * pairs
    chunk = slab_count // blks
    glen = span // blks
    me_blk = lax.axis_index("blk")
    me_pair = lax.axis_index("pair")
    me = me_blk * pairs + me_pair
    lane = lax.broadcasted_iota(jnp.int32, (rows * pairs, width), 1)
    lane_rows = lax.broadcasted_iota(jnp.int32, (rows, width), 1)

    def blk_at(step):
        pattern = blks // 2 + (1 - step % 2) * (step // 2) - (step % 2) * ((step + 1) // 2)
        found, bit = 0, 1
        while bit < blks:
            found = found + lax.rem(me_blk // bit + pattern // bit, 2) * bit
            bit *= 2
        return found

    def ints_copy(step):
        at = blk_at(step)
        return pltpu.make_async_copy(
            ints_hbm.at[pl.ds(at * cap, cap)], ints.at[pl.ds(at * cap, cap)], ints_sem.at[step]
        )

    @pl.loop(0, blks)
    def _(step):
        ints_copy(step).start()

    barrier = pltpu.get_barrier_semaphore()

    @pl.loop(1, devices)
    def _(step):
        other = lax.rem(me + step, devices)
        pl.semaphore_signal(
            barrier,
            inc=1,
            device_id={"blk": other // pairs, "pair": lax.rem(other, pairs)},
            device_id_type=MESH,
        )

    pl.semaphore_wait(barrier, devices - 1)

    def pick_copy(step):
        to = blk_at(step)
        return pltpu.make_async_remote_copy(
            src_ref=picked.at[pl.ds(to * chunk, chunk)],
            dst_ref=picked_in.at[me_blk],
            send_sem=pick_send.at[step],
            recv_sem=pick_recv.at[step],
            device_id={"blk": to},
            device_id_type=MESH,
        )

    @pl.loop(0, blks - 1)
    def _(step):
        pick_copy(step).start()

    @pl.loop(0, blks - 1)
    def _(step):
        pick_copy(step).wait()

    total = picked[pl.ds(me_blk * chunk, chunk)].astype(jnp.float32)
    for step in range(blks - 1):
        total = total + picked_in[blk_at(step)].astype(jnp.float32)
    slab_in[me_pair, me_blk] = total.astype(jnp.bfloat16)

    def gath_copy(step):
        return pltpu.make_async_remote_copy(
            src_ref=slab_in.at[me_pair, me_blk],
            dst_ref=slab_in.at[me_pair, me_blk],
            send_sem=gath_send.at[step],
            recv_sem=gath_recv.at[step],
            device_id={"blk": blk_at(step)},
            device_id_type=MESH,
        )

    def fwd_copy(source_blk, step, turn):
        return pltpu.make_async_remote_copy(
            src_ref=slab_in.at[me_pair, source_blk],
            dst_ref=slab_in.at[me_pair, source_blk],
            send_sem=fwd_send.at[step, turn],
            recv_sem=fwd_recv.at[step, turn],
            device_id={"pair": lax.rem(me_pair + 1 + turn, pairs)},
            device_id_type=MESH,
        )

    @pl.loop(0, blks - 1)
    def _(step):
        gath_copy(step).start()

    for turn in range(pairs - 1):
        fwd_copy(me_blk, blks - 1, turn).start()


    @pl.loop(0, blks - 1)
    def _(step):
        gath_copy(step).wait_recv()
        for turn in range(pairs - 1):
            fwd_copy(blk_at(step), step, turn).start()

    @pl.loop(0, blks - 1)
    def _(step):
        gath_copy(step).wait_send()

    @pl.loop(0, blks)
    def _(step):
        for turn in range(pairs - 1):
            fwd_copy(blk_at(step), step, turn).wait()

    for n in range(slab_count):
        for p in range(pairs):
            slab[
                n // per_irrep,
                p * rows : (p + 1) * rows,
                (n % per_irrep) * width : (n % per_irrep + 1) * width,
            ] = slab_in[p, n // chunk, n % chunk]

    def products(to):
        def slot(r, codes):
            q = to * cap + r
            product = jnp.dot(slab[irrep_ref[to, r]], ints[q], preferred_element_type=jnp.float32)
            largest = jnp.maximum(jnp.max(jnp.abs(product), axis=1, keepdims=True), TINY)
            code = jnp.ceil(jnp.log2(largest) * STEPS)
            scaled = jnp.round(product * (jnp.exp2(code * (-1.0 / STEPS)) * TOP))
            coded = scaled.astype(jnp.int32).astype(jnp.int16)
            for p in range(pairs):
                send1[to * pairs + p, r] = coded[p * rows : (p + 1) * rows]
            return jnp.where(lane == r, code, codes)

        codes = lax.fori_loop(0, cap, slot, jnp.zeros((rows * pairs, width), jnp.float32), unroll=5)
        codes = codes.astype(jnp.int32).astype(jnp.int16)
        for p in range(pairs):
            send1[to * pairs + p, cap] = codes[p * rows : (p + 1) * rows]

    def product_copy(step, turn):
        to = blk_at(step)
        to_pair = lax.rem(me_pair + turn, pairs)
        return pltpu.make_async_remote_copy(
            src_ref=send1.at[to * pairs + to_pair],
            dst_ref=recv1.at[me],
            send_sem=send1_sem.at[step, turn],
            recv_sem=recv1_sem.at[step, turn],
            device_id={"blk": to, "pair": to_pair},
            device_id_type=MESH,
        )

    keep_copy = pltpu.make_async_copy(
        send1.at[me], recv1.at[me], send1_sem.at[blks - 1, 0]
    )

    @pl.loop(0, blks - 1)
    def _(step):
        ints_copy(step).wait()
        products(blk_at(step))
        for turn in range(pairs):
            product_copy(step, turn).start()

    ints_copy(blks - 1).wait()
    products(me_blk)
    keep_copy.start()
    for turn in range(1, pairs):
        product_copy(blks - 1, turn).start()

    keep_copy.wait()

    @pl.loop(0, blks - 1)
    def _(step):
        for turn in range(pairs):
            product_copy(step, turn).wait()

    for turn in range(1, pairs):
        product_copy(blks - 1, turn).wait()

    def code_of(tile, at):
        tile = tile.astype(jnp.int32).astype(jnp.float32)
        return jnp.sum(jnp.where(lane_rows == at, tile, 0.0), axis=1, keepdims=True)

    def value_of(tile, code):
        tile = tile.astype(jnp.int32).astype(jnp.float32)
        return tile * (jnp.exp2(code * (1.0 / STEPS)) * (1.0 / TOP))

    def mirror_copy(step):
        to = blk_at(step)
        return pltpu.make_async_remote_copy(
            src_ref=send2.at[to],
            dst_ref=recv2.at[me_blk],
            send_sem=send2_sem.at[step],
            recv_sem=recv2_sem.at[step],
            device_id={"blk": to, "pair": lax.rem(me_pair + pairs // 2, pairs)},
            device_id_type=MESH,
        )

    @pl.loop(0, blks)
    def _(step):
        to = blk_at(step)

        def entry(m, codes):
            dev = meta_ref[2, to * glen + m]
            rank = meta_ref[3, to * glen + m]
            send2[to, m] = recv1[dev, rank]
            return jnp.where(lane_rows == m, code_of(recv1[dev, cap], rank), codes)

        codes = lax.fori_loop(0, glen, entry, jnp.zeros((rows, width), jnp.float32), unroll=8)
        send2[to, glen] = codes.astype(jnp.int32).astype(jnp.int16)
        mirror_copy(step).start()

    def own_entry(i, carry):
        dev = meta_ref[0, i]
        rank = meta_ref[1, i]
        own[i] = value_of(recv1[dev, rank], code_of(recv1[dev, cap], rank))
        return carry

    lax.fori_loop(0, span, own_entry, 0, unroll=8)

    @pl.loop(0, blks)
    def _(step):
        mirror_copy(step).wait()
        source = blk_at(step)
        codes = recv2[source, glen]

        def entry(m, carry):
            facing[source, m] = value_of(recv2[source, m], code_of(codes, m))
            return carry

        lax.fori_loop(0, glen, entry, 0, unroll=8)

    def out_entry(i, carry):
        mirrored = facing[meta_ref[4, i], meta_ref[5, i]]
        total = own[i] + meta_ref[6, i].astype(jnp.float32) * mirrored
        out_ref[:, pl.ds(pl.multiple_of(i * width, width), width)] = total.astype(jnp.bfloat16)
        return carry

    lax.fori_loop(0, span, out_entry, 0, unroll=8)


def local(amplitudes, integrals, block_irrep, slab_blocks, owner, partner, sign):
    rows, columns = amplitudes.shape
    slots, per_irrep, _, width = integrals.shape
    blks = lax.axis_size("blk")
    pairs = lax.axis_size("pair")
    devices = blks * pairs
    span = columns // width
    cap = slots // blks
    glen = span // blks
    slab_count = slab_blocks.shape[0]
    irreps = slab_count // per_irrep
    chunk = slab_count // blks
    inner = per_irrep * width
    tables = [table.reshape(-1, width) for table in (owner, partner, block_irrep, sign)]

    sizes = (blks, pairs, span, cap, per_irrep, slab_count, rows, width)
    smem = pl.BlockSpec(memory_space=pltpu.SMEM)
    vmem = pl.BlockSpec(memory_space=pltpu.VMEM)
    dma = pltpu.SemaphoreType.DMA
    hbm = pl.BlockSpec(memory_space=pl.ANY)
    slot_irrep, meta, picked = pl.pallas_call(
        functools.partial(prep_kernel, sizes),
        out_shape=(
            jax.ShapeDtypeStruct((blks, width), jnp.int32),
            jax.ShapeDtypeStruct((8, span), jnp.int32),
            jax.ShapeDtypeStruct((slab_count, rows, width), jnp.bfloat16),
        ),
        in_specs=[smem] + [vmem] * 4 + [hbm],
        out_specs=(vmem, vmem, vmem),
        scratch_shapes=[
            pltpu.VMEM((slab_count, rows, width), jnp.bfloat16),
            dma((slab_count,)),
        ],
    )(slab_blocks, *tables, amplitudes)
    return pl.pallas_call(
        functools.partial(kernel, sizes),
        out_shape=jax.ShapeDtypeStruct((rows, columns), jnp.bfloat16),
        in_specs=[smem, smem, vmem, hbm],
        out_specs=vmem,
        scratch_shapes=[
            pltpu.VMEM((slots, inner, width), jnp.bfloat16),
            pltpu.VMEM((blks, chunk, rows, width), jnp.bfloat16),
            pltpu.VMEM((pairs, blks, chunk, rows, width), jnp.bfloat16),
            pltpu.VMEM((irreps, rows * pairs, inner), jnp.bfloat16),
            pltpu.VMEM((devices, cap + 1, rows, width), jnp.int16),
            pltpu.VMEM((devices, cap + 1, rows, width), jnp.int16),
            pltpu.VMEM((span, rows, width), jnp.float32),
            pltpu.VMEM((blks, glen + 1, rows, width), jnp.int16),
            pltpu.VMEM((blks, glen + 1, rows, width), jnp.int16),
            pltpu.VMEM((blks, glen, rows, width), jnp.float32),
            dma((blks,)),
            dma((blks,)),
            dma((blks,)),
            dma((blks,)),
            dma((blks,)),
            dma((blks, pairs)),
            dma((blks, pairs)),
            dma((blks, pairs)),
            dma((blks, pairs)),
            dma((blks,)),
            dma((blks,)),
        ],
        compiler_params=pltpu.CompilerParams(
            collective_id=0, has_side_effects=True, vmem_limit_bytes=56 * 2**20
        ),
    )(
        slot_irrep,
        meta,
        picked,
        integrals.reshape(slots, inner, width),
    )


def solution(mesh):
    placed = (P("pair", "blk"), P(("blk", "pair"), None, None, None), P(), P(), P(), P(), P())
    return jax.shard_map(
        local, mesh=mesh, in_specs=placed, out_specs=P("pair", "blk"), check_vma=False
    )
```

profile of v0, /device:TPU:13, one launch (start us, length us, event | category | flops | bytes accessed | tf_op | source)
XLA Modules:
  0.0 122.5 jit_solution(1031926435609382772)
XLA Ops:
  0.0 3.5 %shard_map.73 = (s32[8,128]{1,0:T(8,128)}, s32[8,256]{1,0:T(8,128)}, bf16[32,16,128]{2,1,0:T(8,128)(2,1)}) custom-call(s32[32]{0:T(128)} %slab_ref.1, s32[16,128]{1,0:T(8,128)} %bitcast.6, s32[16,128]{1,0:T(8,128)} %bitcast.7, s32[16,128]{1,0:T(8,128)} %bitcast.8, s32[16,128]{1,0:T(8,128)} %bitcast.9, bf16[16,32768]{1,0:T(8,128)(2,1)} %amp_hbm.1), custom_call_target="tpu_custom_call" | custom-call | tf_op jit(solution)/shard_map/pallas_call | solution.py:388
  3.5 116.8 %shard_map.74 = bf16[16,32768]{1,0:T(8,128)(2,1)} custom-call(s32[8,128]{1,0:T(8,128)} %get-tuple-element.8.irrep_ref, s32[8,256]{1,0:T(8,128)} %get-tuple-element.9.meta_ref, bf16[32,16,128]{2,1,0:T(8,128)(2,1)} %get-tuple-element.10.picked, bf16[160,512,128]{2,1,0:T(8,128)(2,1)} %bitcast.5), custom_call_target="tpu_custom_call" | custom-call | tf_op jit(solution)/shard_map/pallas_call | solution.py:402
  120.3 2.3 %copy.9 = bf16[16,32768]{1,0:T(8,128)(2,1)} copy(bf16[16,32768]{1,0:T(8,128)(2,1)} %shard_map.74) | data formatting | bytes 2097152
where the time goes:
time: 125 us; the launch traced here: 123 us
  Pallas kernels  120 us (96%)
  local copies, waits for them, and re-layouts  2.26 us (2%)
    pallas_call x1, Pallas kernels, local(): pl.pallas_call(functools.partial(kernel, sizes), out_shape=jax.ShapeDtype...  117 us
    pallas_call x1, Pallas kernels, local(): pl.pallas_call(functools.partial(prep_kernel, sizes), out_shape=(jax.Shap...  3.47 us

commit v1 on v0

--- a/solution.py
+++ b/solution.py
@@ -8,9 +8,13 @@
 from jax.sharding import PartitionSpec as P
 
 TOP = 32766.0
-STEPS = 256.0
-TINY = 2.0**-120
+TINY = 2.0**-110
 MESH = pl.DeviceIdType.MESH
+HALVES = 2
+
+
+def unroll_of(trips, most):
+    return max(n for n in range(1, most + 1) if trips % n == 0)
 
 
 def prep_kernel(
@@ -75,7 +79,17 @@
     key_col = column(send_key)
     send_dev = placed(key_col, owner_col)
     send_rank = placed(key_col, column(rank))
-    for at, row in enumerate((owner, rank, send_dev, send_rank, partner_blk, mirror_rank, sign)):
+    capw, glenw = -(-cap // 2), span // blks // 2
+    table = []
+    for index, count_of, place in (
+        (owner, capw, rank),
+        (send_dev, capw, send_rank),
+        (partner_blk, glenw, mirror_rank),
+    ):
+        word = jnp.floor(place * 0.5)
+        shift = 16.0 - 16.0 * (place - 2.0 * word)
+        table += [index, place, index * count_of + word, shift]
+    for at, row in enumerate(table + [sign]):
         meta_out[at : at + 1, :] = row.astype(jnp.int32)
 
     stored = every(owner_ref) == me
@@ -112,12 +126,22 @@
     picked_in,
     slab_in,
     slab,
-    send1,
-    recv1,
+    send1a,
+    send1b,
+    recv1a,
+    recv1b,
+    scale1,
+    scale1_in,
+    scale1_s,
     own,
-    send2,
-    recv2,
-    facing,
+    send2a,
+    send2b,
+    recv2a,
+    recv2b,
+    scale2_s,
+    scale2,
+    scale2_in,
+    scale2_in_s,
     ints_sem,
     pick_send,
     pick_recv,
@@ -129,6 +153,7 @@
     recv1_sem,
     send2_sem,
     recv2_sem,
+    table_sem,
 ):
     blks, pairs, span, cap, per_irrep, slab_count, rows, width = sizes
     devices = blks * pairs
@@ -137,8 +162,10 @@
     me_blk = lax.axis_index("blk")
     me_pair = lax.axis_index("pair")
     me = me_blk * pairs + me_pair
-    lane = lax.broadcasted_iota(jnp.int32, (rows * pairs, width), 1)
-    lane_rows = lax.broadcasted_iota(jnp.int32, (rows, width), 1)
+    capw, glenw, half = -(-cap // 2), glen // 2, rows // 2
+    lane = lax.broadcasted_iota(jnp.int32, (1, width), 1)
+    send1, recv1 = (send1a, send1b), (recv1a, recv1b)
+    send2, recv2 = (send2a, send2b), (recv2a, recv2b)
 
     def blk_at(step):
         pattern = blks // 2 + (1 - step % 2) * (step // 2) - (step % 2) * ((step + 1) // 2)
@@ -248,121 +275,185 @@
             ] = slab_in[p, n // chunk, n % chunk]
 
     def products(to):
-        def slot(r, codes):
-            q = to * cap + r
-            product = jnp.dot(slab[irrep_ref[to, r]], ints[q], preferred_element_type=jnp.float32)
-            largest = jnp.maximum(jnp.max(jnp.abs(product), axis=1, keepdims=True), TINY)
-            code = jnp.ceil(jnp.log2(largest) * STEPS)
-            scaled = jnp.round(product * (jnp.exp2(code * (-1.0 / STEPS)) * TOP))
-            coded = scaled.astype(jnp.int32).astype(jnp.int16)
+        def slots(j, scales):
+            coded = []
+            for turn in range(2):
+                r = jnp.minimum(2 * j + turn, cap - 1)
+                product = jnp.dot(
+                    slab[irrep_ref[to, r]], ints[to * cap + r], preferred_element_type=jnp.float32
+                )
+                tiles, found = [], []
+                for p in range(pairs):
+                    tile = product[p * rows : (p + 1) * rows]
+                    largest = jnp.max(jnp.abs(tile), axis=0, keepdims=True)
+                    largest = jnp.maximum(jnp.max(largest, axis=1, keepdims=True), TINY)
+                    tiles.append(jnp.round(tile * (TOP / largest)).astype(jnp.int32))
+                    found.append(jnp.where(lane == r, largest * (1.0 / TOP), scales[p]))
+                scales = tuple(found)
+                coded.append(tiles)
             for p in range(pairs):
-                send1[to * pairs + p, r] = coded[p * rows : (p + 1) * rows]
-            return jnp.where(lane == r, code, codes)
-
-        codes = lax.fori_loop(0, cap, slot, jnp.zeros((rows * pairs, width), jnp.float32), unroll=5)
-        codes = codes.astype(jnp.int32).astype(jnp.int16)
+                word = (coded[0][p] & 0xFFFF) | (coded[1][p] << 16)
+                for h in range(HALVES):
+                    send1[h][(to * pairs + p) * capw + j] = word[h * half : (h + 1) * half]
+            return scales
+
+        start = tuple(jnp.zeros((1, width), jnp.float32) for _ in range(pairs))
+        scales = lax.fori_loop(0, capw, slots, start, unroll=unroll_of(capw, 5))
         for p in range(pairs):
-            send1[to * pairs + p, cap] = codes[p * rows : (p + 1) * rows]
-
-    def product_copy(step, turn):
+            scale1[to * pairs + p] = scales[p]
+
+    def product_copy(h, step, turn):
         to = blk_at(step)
         to_pair = lax.rem(me_pair + turn, pairs)
+        at = to * pairs + to_pair
+        if h == HALVES:
+            source, target = scale1.at[at], scale1_in.at[me]
+        else:
+            source = send1[h].at[pl.ds(at * capw, capw)]
+            target = recv1[h].at[pl.ds(me * capw, capw)]
         return pltpu.make_async_remote_copy(
-            src_ref=send1.at[to * pairs + to_pair],
-            dst_ref=recv1.at[me],
-            send_sem=send1_sem.at[step, turn],
-            recv_sem=recv1_sem.at[step, turn],
+            src_ref=source,
+            dst_ref=target,
+            send_sem=send1_sem.at[h, step, turn],
+            recv_sem=recv1_sem.at[h, step, turn],
             device_id={"blk": to, "pair": to_pair},
             device_id_type=MESH,
         )
 
-    keep_copy = pltpu.make_async_copy(
-        send1.at[me], recv1.at[me], send1_sem.at[blks - 1, 0]
-    )
+    def keep_copy(h):
+        if h == HALVES:
+            source, target = scale1.at[me], scale1_in.at[me]
+        else:
+            source = send1[h].at[pl.ds(me * capw, capw)]
+            target = recv1[h].at[pl.ds(me * capw, capw)]
+        return pltpu.make_async_copy(source, target, send1_sem.at[h, blks - 1, 0])
+
+    def send_products(h):
+        @pl.loop(0, blks - 1)
+        def _(step):
+            for turn in range(pairs):
+                product_copy(h, step, turn).start()
+
+        keep_copy(h).start()
+        for turn in range(1, pairs):
+            product_copy(h, blks - 1, turn).start()
+
+    def wait_products(h):
+        keep_copy(h).wait()
+
+        @pl.loop(0, blks - 1)
+        def _(step):
+            for turn in range(pairs):
+                product_copy(h, step, turn).wait()
+
+        for turn in range(1, pairs):
+            product_copy(h, blks - 1, turn).wait()
 
     @pl.loop(0, blks - 1)
     def _(step):
         ints_copy(step).wait()
         products(blk_at(step))
-        for turn in range(pairs):
-            product_copy(step, turn).start()
+        for h in (HALVES, 0):
+            for turn in range(pairs):
+                product_copy(h, step, turn).start()
 
     ints_copy(blks - 1).wait()
     products(me_blk)
-    keep_copy.start()
-    for turn in range(1, pairs):
-        product_copy(blks - 1, turn).start()
-
-    keep_copy.wait()
-
-    @pl.loop(0, blks - 1)
-    def _(step):
-        for turn in range(pairs):
-            product_copy(step, turn).wait()
-
-    for turn in range(1, pairs):
-        product_copy(blks - 1, turn).wait()
-
-    def code_of(tile, at):
-        tile = tile.astype(jnp.int32).astype(jnp.float32)
-        return jnp.sum(jnp.where(lane_rows == at, tile, 0.0), axis=1, keepdims=True)
-
-    def value_of(tile, code):
-        tile = tile.astype(jnp.int32).astype(jnp.float32)
-        return tile * (jnp.exp2(code * (1.0 / STEPS)) * (1.0 / TOP))
-
-    def mirror_copy(step):
+    for h in (HALVES, 0):
+        keep_copy(h).start()
+        for turn in range(1, pairs):
+            product_copy(h, blks - 1, turn).start()
+    send_products(1)
+
+    def mirror_copy(h, step):
         to = blk_at(step)
+        if h == HALVES:
+            source, target = scale2.at[to], scale2_in.at[me_blk]
+        else:
+            source = send2[h].at[pl.ds(to * glenw, glenw)]
+            target = recv2[h].at[pl.ds(me_blk * glenw, glenw)]
         return pltpu.make_async_remote_copy(
-            src_ref=send2.at[to],
-            dst_ref=recv2.at[me_blk],
-            send_sem=send2_sem.at[step],
-            recv_sem=recv2_sem.at[step],
+            src_ref=source,
+            dst_ref=target,
+            send_sem=send2_sem.at[h, step],
+            recv_sem=recv2_sem.at[h, step],
             device_id={"blk": to, "pair": lax.rem(me_pair + pairs // 2, pairs)},
             device_id_type=MESH,
         )
 
+    def table_copy(source, target, at):
+        return pltpu.make_async_copy(source, target, table_sem.at[at])
+
+    def value_of(word, shift):
+        return ((word << shift) >> 16).astype(jnp.float32)
+
+    def gather(h):
+        @pl.loop(0, blks)
+        def _(step):
+            to = blk_at(step)
+
+            def entry(m, carry):
+                i = to * glen + 2 * m
+                low = recv1[h][meta_ref[6, i]] << meta_ref[7, i]
+                high = recv1[h][meta_ref[6, i + 1]] << meta_ref[7, i + 1]
+                send2[h][to * glenw + m] = lax.shift_right_logical(low, 16) | (high & -65536)
+                return carry
+
+            lax.fori_loop(0, glenw, entry, 0, unroll=unroll_of(glenw, 8))
+            mirror_copy(h, step).start()
+
+        def own_entry(i, carry):
+            scale = scale1_s[meta_ref[0, i], 0, meta_ref[1, i]]
+            own[h, i] = value_of(recv1[h][meta_ref[2, i]], meta_ref[3, i]) * scale
+            return carry
+
+        lax.fori_loop(0, span, own_entry, 0, unroll=unroll_of(span, 8))
+
+    def finish(h):
+        def out_entry(i, carry):
+            scale = scale2_in_s[meta_ref[8, i], 0, meta_ref[9, i]] * meta_ref[12, i].astype(jnp.float32)
+            mirrored = value_of(recv2[h][meta_ref[10, i]], meta_ref[11, i])
+            total = own[h, i] + mirrored * scale
+            columns = pl.ds(pl.multiple_of(i * width, width), width)
+            out_ref[h * half : (h + 1) * half, columns] = total.astype(jnp.bfloat16)
+            return carry
+
+        lax.fori_loop(0, span, out_entry, 0, unroll=unroll_of(span, 8))
+
+    wait_products(HALVES)
+    table_copy(scale1_in, scale1_s, 0).start()
+    table_copy(scale1_in, scale1_s, 0).wait()
+
+    def scale_entry(i, carry):
+        scale2_s[i // glen, 0, i % glen] = scale1_s[meta_ref[4, i], 0, meta_ref[5, i]]
+        return carry
+
+    lax.fori_loop(0, span, scale_entry, 0, unroll=unroll_of(span, 8))
+    table_copy(scale2_s, scale2, 1).start()
+    table_copy(scale2_s, scale2, 1).wait()
+
     @pl.loop(0, blks)
     def _(step):
-        to = blk_at(step)
-
-        def entry(m, codes):
-            dev = meta_ref[2, to * glen + m]
-            rank = meta_ref[3, to * glen + m]
-            send2[to, m] = recv1[dev, rank]
-            return jnp.where(lane_rows == m, code_of(recv1[dev, cap], rank), codes)
-
-        codes = lax.fori_loop(0, glen, entry, jnp.zeros((rows, width), jnp.float32), unroll=8)
-        send2[to, glen] = codes.astype(jnp.int32).astype(jnp.int16)
-        mirror_copy(step).start()
-
-    def own_entry(i, carry):
-        dev = meta_ref[0, i]
-        rank = meta_ref[1, i]
-        own[i] = value_of(recv1[dev, rank], code_of(recv1[dev, cap], rank))
-        return carry
-
-    lax.fori_loop(0, span, own_entry, 0, unroll=8)
+        mirror_copy(HALVES, step).start()
+
+    wait_products(0)
+    gather(0)
 
     @pl.loop(0, blks)
     def _(step):
-        mirror_copy(step).wait()
-        source = blk_at(step)
-        codes = recv2[source, glen]
-
-        def entry(m, carry):
-            facing[source, m] = value_of(recv2[source, m], code_of(codes, m))
-            return carry
-
-        lax.fori_loop(0, glen, entry, 0, unroll=8)
-
-    def out_entry(i, carry):
-        mirrored = facing[meta_ref[4, i], meta_ref[5, i]]
-        total = own[i] + meta_ref[6, i].astype(jnp.float32) * mirrored
-        out_ref[:, pl.ds(pl.multiple_of(i * width, width), width)] = total.astype(jnp.bfloat16)
-        return carry
-
-    lax.fori_loop(0, span, out_entry, 0, unroll=8)
+        mirror_copy(HALVES, step).wait()
+
+    table_copy(scale2_in, scale2_in_s, 2).start()
+    table_copy(scale2_in, scale2_in_s, 2).wait()
+    wait_products(1)
+    gather(1)
+    for h in range(HALVES):
+
+        @pl.loop(0, blks)
+        def _(step):
+            mirror_copy(h, step).wait()
+
+        finish(h)
 
 
 def local(amplitudes, integrals, block_irrep, slab_blocks, owner, partner, sign):
@@ -378,6 +469,7 @@
     irreps = slab_count // per_irrep
     chunk = slab_count // blks
     inner = per_irrep * width
+    capw, half = -(-cap // 2), rows // 2
     tables = [table.reshape(-1, width) for table in (owner, partner, block_irrep, sign)]
 
     sizes = (blks, pairs, span, cap, per_irrep, slab_count, rows, width)
@@ -389,7 +481,7 @@
         functools.partial(prep_kernel, sizes),
         out_shape=(
             jax.ShapeDtypeStruct((blks, width), jnp.int32),
-            jax.ShapeDtypeStruct((8, span), jnp.int32),
+            jax.ShapeDtypeStruct((16, span), jnp.int32),
             jax.ShapeDtypeStruct((slab_count, rows, width), jnp.bfloat16),
         ),
         in_specs=[smem] + [vmem] * 4 + [hbm],
@@ -409,12 +501,16 @@
             pltpu.VMEM((blks, chunk, rows, width), jnp.bfloat16),
             pltpu.VMEM((pairs, blks, chunk, rows, width), jnp.bfloat16),
             pltpu.VMEM((irreps, rows * pairs, inner), jnp.bfloat16),
-            pltpu.VMEM((devices, cap + 1, rows, width), jnp.int16),
-            pltpu.VMEM((devices, cap + 1, rows, width), jnp.int16),
-            pltpu.VMEM((span, rows, width), jnp.float32),
-            pltpu.VMEM((blks, glen + 1, rows, width), jnp.int16),
-            pltpu.VMEM((blks, glen + 1, rows, width), jnp.int16),
-            pltpu.VMEM((blks, glen, rows, width), jnp.float32),
+            *[pltpu.VMEM((devices * capw, half, width), jnp.int32)] * 4,
+            pltpu.VMEM((devices, 1, width), jnp.float32),
+            pltpu.VMEM((devices, 1, width), jnp.float32),
+            pltpu.SMEM((devices, 1, width), jnp.float32),
+            pltpu.VMEM((HALVES, span, half, width), jnp.float32),
+            *[pltpu.VMEM((span // 2, half, width), jnp.int32)] * 4,
+            pltpu.SMEM((blks, 1, width), jnp.float32),
+            pltpu.VMEM((blks, 1, width), jnp.float32),
+            pltpu.VMEM((blks, 1, width), jnp.float32),
+            pltpu.SMEM((blks, 1, width), jnp.float32),
             dma((blks,)),
             dma((blks,)),
             dma((blks,)),
@@ -422,10 +518,11 @@
             dma((blks,)),
             dma((blks, pairs)),
             dma((blks, pairs)),
-            dma((blks, pairs)),
-            dma((blks, pairs)),
-            dma((blks,)),
-            dma((blks,)),
+            dma((HALVES + 1, blks, pairs)),
+            dma((HALVES + 1, blks, pairs)),
+            dma((HALVES + 1, blks)),
+            dma((HALVES + 1, blks)),
+            dma((3,)),
         ],
         compiler_params=pltpu.CompilerParams(
             collective_id=0, has_side_effects=True, vmem_limit_bytes=56 * 2**20

time: 125 us -> 117 us (0.936); the launches traced: 123 us -> 117 us
  Pallas kernels: 120 us -> 114 us
    pallas_call x1, Pallas kernels: 117 us -> 111 us  [local(): pl.pallas_call(functools.partial(kernel, sizes), out_shape=jax.ShapeDtype...]
where the time goes in v1:
time: 117 us
  Pallas kernels  114 us (97%)
  local copies, waits for them, and re-layouts  2.26 us (2%)
    pallas_call x1, Pallas kernels, local(): pl.pallas_call(functools.partial(kernel, sizes), out_shape=jax.ShapeDtype...  111 us
    pallas_call x1, Pallas kernels, local(): pl.pallas_call(functools.partial(prep_kernel, sizes), out_shape=(jax.Shap...  3.67 us

profile of v1, /device:TPU:13, one launch (start us, length us, event | category | flops | bytes accessed | tf_op | source)
XLA Modules:
  0.0 116.6 jit_solution(251182940052210245)
XLA Ops:
  0.0 3.7 %shard_map.73 = (s32[8,128]{1,0:T(8,128)}, s32[16,256]{1,0:T(8,128)}, bf16[32,16,128]{2,1,0:T(8,128)(2,1)}) custom-call(s32[32]{0:T(128)} %slab_ref.1, s32[16,128]{1,0:T(8,128)} %bitcast.6, s32[16,128]{1,0:T(8,128)} %bitcast.7, s32[16,128]{1,0:T(8,128)} %bitcast.8, s32[16,128]{1,0:T(8,128)} %bitcast.9, bf16[16,32768]{1,0:T(8,128)(2,1)} %amp_hbm.1), custom_call_target="tpu_custom_call" | custom-call | tf_op jit(solution)/shard_map/pallas_call | solution.py:480
  3.7 110.6 %shard_map.74 = bf16[16,32768]{1,0:T(8,128)(2,1)} custom-call(s32[8,128]{1,0:T(8,128)} %get-tuple-element.8.irrep_ref, s32[16,256]{1,0:T(8,128)} %get-tuple-element.9.meta_ref, bf16[32,16,128]{2,1,0:T(8,128)(2,1)} %get-tuple-element.10.picked, bf16[160,512,128]{2,1,0:T(8,128)(2,1)} %bitcast.5), custom_call_target="tpu_custom_call" | custom-call | tf_op jit(solution)/shard_map/pallas_call | solution.py:494
  114.3 2.3 %copy.9 = bf16[16,32768]{1,0:T(8,128)(2,1)} copy(bf16[16,32768]{1,0:T(8,128)(2,1)} %shard_map.74) | data formatting | bytes 2097152

commit v2 on v1

--- a/solution.py
+++ b/solution.py
@@ -17,32 +17,10 @@
     return max(n for n in range(1, most + 1) if trips % n == 0)
 
 
-def prep_kernel(
-    sizes,
-    slab_ref,
-    owner_ref,
-    partner_ref,
-    irrep_ref,
-    sign_ref,
-    amp_hbm,
-    irrep_out,
-    meta_out,
-    picked,
-    raw,
-    pick_sem,
-):
+def fill_tables(sizes, owner_ref, partner_ref, irrep_ref, sign_ref, irrep_out, meta_out):
     blks, pairs, span, cap, per_irrep, slab_count, rows, width = sizes
     me_blk = lax.axis_index("blk")
     me = me_blk * pairs + lax.axis_index("pair")
-
-    def pick(n):
-        at = jnp.clip(slab_ref[n] - me_blk * span, 0, span - 1) * width
-        return pltpu.make_async_copy(
-            amp_hbm.at[:, pl.ds(pl.multiple_of(at, width), width)], raw.at[n], pick_sem.at[n]
-        )
-
-    for n in range(slab_count):
-        pick(n).start()
 
     down = lax.broadcasted_iota(jnp.int32, (span, span), 0)
     across = lax.broadcasted_iota(jnp.int32, (span, span), 1)
@@ -66,7 +44,10 @@
         return jnp.concatenate(found, axis=1).astype(jnp.float32)
 
     def every(ref):
-        found = [ref[pl.ds(part, blks, stride=parts), :] for part in range(parts)]
+        found = [
+            jnp.concatenate([ref[b * parts + part : b * parts + part + 1, :] for b in range(blks)])
+            for part in range(parts)
+        ]
         return jnp.concatenate(found, axis=1)
 
     owner, partner, sign = mine(owner_ref), mine(partner_ref), mine(sign_ref)
@@ -81,11 +62,13 @@
     send_rank = placed(key_col, column(rank))
     capw, glenw = -(-cap // 2), span // blks // 2
     table = []
-    for index, count_of, place in (
-        (owner, capw, rank),
-        (send_dev, capw, send_rank),
-        (partner_blk, glenw, mirror_rank),
+    for index, most, count_of, place in (
+        (owner, blks * pairs, capw, rank),
+        (send_dev, blks * pairs, capw, send_rank),
+        (partner_blk, blks, glenw, mirror_rank),
     ):
+        index = jnp.clip(index, 0.0, most - 1.0)
+        place = jnp.clip(place, 0.0, min(2 * count_of, width) - 1.0)
         word = jnp.floor(place * 0.5)
         shift = 16.0 - 16.0 * (place - 2.0 * word)
         table += [index, place, index * count_of + word, shift]
@@ -107,21 +90,24 @@
         slots = jnp.where(lane == r, found, slots)
     irrep_out[...] = slots.astype(jnp.int32)
 
-    for n in range(slab_count):
-        pick(n).wait()
-    for n in range(slab_count):
-        local = slab_ref[n] - me_blk * span
-        inside = jnp.logical_and(local >= 0, local < span).astype(jnp.float32)
-        picked[n] = (raw[n].astype(jnp.float32) * inside).astype(jnp.bfloat16)
-
 
 def kernel(
     sizes,
+    slab_ref,
+    owner_ref,
+    partner_ref,
+    irreps_ref,
+    sign_ref,
+    amp_hbm,
+    ints_hbm,
+    out_ref,
+    amp,
+    amp_blocks,
+    picked,
+    irrep_v,
+    meta_v,
     irrep_ref,
     meta_ref,
-    picked,
-    ints_hbm,
-    out_ref,
     ints,
     picked_in,
     slab_in,
@@ -181,6 +167,11 @@
             ints_hbm.at[pl.ds(at * cap, cap)], ints.at[pl.ds(at * cap, cap)], ints_sem.at[step]
         )
 
+    def table_copy(source, target, at):
+        return pltpu.make_async_copy(source, target, table_sem.at[at])
+
+    table_copy(amp_hbm, amp, 0).start()
+
     @pl.loop(0, blks)
     def _(step):
         ints_copy(step).start()
@@ -196,6 +187,19 @@
             device_id={"blk": other // pairs, "pair": lax.rem(other, pairs)},
             device_id_type=MESH,
         )
+
+    table_copy(amp_hbm, amp, 0).wait()
+
+    def split(i, carry):
+        amp_blocks[i] = amp[:, pl.ds(pl.multiple_of(i * width, width), width)]
+        return carry
+
+    lax.fori_loop(0, span, split, 0, unroll=unroll_of(span, 8))
+    for n in range(slab_count):
+        local = slab_ref[n] - me_blk * span
+        inside = jnp.logical_and(local >= 0, local < span).astype(jnp.float32)
+        block = amp_blocks[jnp.clip(local, 0, span - 1)]
+        picked[n] = (block.astype(jnp.float32) * inside).astype(jnp.bfloat16)
 
     pl.semaphore_wait(barrier, devices - 1)
 
@@ -214,6 +218,10 @@
     def _(step):
         pick_copy(step).start()
 
+    fill_tables(sizes, owner_ref, partner_ref, irreps_ref, sign_ref, irrep_v, meta_v)
+    table_copy(irrep_v, irrep_ref, 1).start()
+    table_copy(meta_v, meta_ref, 2).start()
+
     @pl.loop(0, blks - 1)
     def _(step):
         pick_copy(step).wait()
@@ -274,13 +282,16 @@
                 (n % per_irrep) * width : (n % per_irrep + 1) * width,
             ] = slab_in[p, n // chunk, n % chunk]
 
+    table_copy(irrep_v, irrep_ref, 1).wait()
+    table_copy(meta_v, meta_ref, 2).wait()
+
     def products(to):
         def slots(j, scales):
             coded = []
             for turn in range(2):
                 r = jnp.minimum(2 * j + turn, cap - 1)
                 product = jnp.dot(
-                    slab[irrep_ref[to, r]], ints[to * cap + r], preferred_element_type=jnp.float32
+                    slab[jnp.clip(irrep_ref[to, r], 0, slab_count // per_irrep - 1)], ints[to * cap + r], preferred_element_type=jnp.float32
                 )
                 tiles, found = [], []
                 for p in range(pairs):
@@ -381,9 +392,6 @@
             device_id_type=MESH,
         )
 
-    def table_copy(source, target, at):
-        return pltpu.make_async_copy(source, target, table_sem.at[at])
-
     def value_of(word, shift):
         return ((word << shift) >> 16).astype(jnp.float32)
 
@@ -394,8 +402,8 @@
 
             def entry(m, carry):
                 i = to * glen + 2 * m
-                low = recv1[h][meta_ref[6, i]] << meta_ref[7, i]
-                high = recv1[h][meta_ref[6, i + 1]] << meta_ref[7, i + 1]
+                low = recv1[h][jnp.clip(meta_ref[6, i], 0, devices * capw - 1)] << meta_ref[7, i]
+                high = recv1[h][jnp.clip(meta_ref[6, i + 1], 0, devices * capw - 1)] << meta_ref[7, i + 1]
                 send2[h][to * glenw + m] = lax.shift_right_logical(low, 16) | (high & -65536)
                 return carry
 
@@ -403,16 +411,16 @@
             mirror_copy(h, step).start()
 
         def own_entry(i, carry):
-            scale = scale1_s[meta_ref[0, i], 0, meta_ref[1, i]]
-            own[h, i] = value_of(recv1[h][meta_ref[2, i]], meta_ref[3, i]) * scale
+            scale = scale1_s[jnp.clip(meta_ref[0, i], 0, devices - 1), 0, jnp.clip(meta_ref[1, i], 0, width - 1)]
+            own[h, i] = value_of(recv1[h][jnp.clip(meta_ref[2, i], 0, devices * capw - 1)], meta_ref[3, i]) * scale
             return carry
 
         lax.fori_loop(0, span, own_entry, 0, unroll=unroll_of(span, 8))
 
     def finish(h):
         def out_entry(i, carry):
-            scale = scale2_in_s[meta_ref[8, i], 0, meta_ref[9, i]] * meta_ref[12, i].astype(jnp.float32)
-            mirrored = value_of(recv2[h][meta_ref[10, i]], meta_ref[11, i])
+            scale = scale2_in_s[jnp.clip(meta_ref[8, i], 0, blks - 1), 0, jnp.clip(meta_ref[9, i], 0, width - 1)] * meta_ref[12, i].astype(jnp.float32)
+            mirrored = value_of(recv2[h][jnp.clip(meta_ref[10, i], 0, span // 2 - 1)], meta_ref[11, i])
             total = own[h, i] + mirrored * scale
             columns = pl.ds(pl.multiple_of(i * width, width), width)
             out_ref[h * half : (h + 1) * half, columns] = total.astype(jnp.bfloat16)
@@ -421,16 +429,16 @@
         lax.fori_loop(0, span, out_entry, 0, unroll=unroll_of(span, 8))
 
     wait_products(HALVES)
-    table_copy(scale1_in, scale1_s, 0).start()
-    table_copy(scale1_in, scale1_s, 0).wait()
+    table_copy(scale1_in, scale1_s, 3).start()
+    table_copy(scale1_in, scale1_s, 3).wait()
 
     def scale_entry(i, carry):
-        scale2_s[i // glen, 0, i % glen] = scale1_s[meta_ref[4, i], 0, meta_ref[5, i]]
+        scale2_s[i // glen, 0, i % glen] = scale1_s[jnp.clip(meta_ref[4, i], 0, devices - 1), 0, jnp.clip(meta_ref[5, i], 0, width - 1)]
         return carry
 
     lax.fori_loop(0, span, scale_entry, 0, unroll=unroll_of(span, 8))
-    table_copy(scale2_s, scale2, 1).start()
-    table_copy(scale2_s, scale2, 1).wait()
+    table_copy(scale2_s, scale2, 4).start()
+    table_copy(scale2_s, scale2, 4).wait()
 
     @pl.loop(0, blks)
     def _(step):
@@ -443,8 +451,8 @@
     def _(step):
         mirror_copy(HALVES, step).wait()
 
-    table_copy(scale2_in, scale2_in_s, 2).start()
-    table_copy(scale2_in, scale2_in_s, 2).wait()
+    table_copy(scale2_in, scale2_in_s, 5).start()
+    table_copy(scale2_in, scale2_in_s, 5).wait()
     wait_products(1)
     gather(1)
     for h in range(HALVES):
@@ -477,26 +485,19 @@
     vmem = pl.BlockSpec(memory_space=pltpu.VMEM)
     dma = pltpu.SemaphoreType.DMA
     hbm = pl.BlockSpec(memory_space=pl.ANY)
-    slot_irrep, meta, picked = pl.pallas_call(
-        functools.partial(prep_kernel, sizes),
-        out_shape=(
-            jax.ShapeDtypeStruct((blks, width), jnp.int32),
-            jax.ShapeDtypeStruct((16, span), jnp.int32),
-            jax.ShapeDtypeStruct((slab_count, rows, width), jnp.bfloat16),
-        ),
-        in_specs=[smem] + [vmem] * 4 + [hbm],
-        out_specs=(vmem, vmem, vmem),
-        scratch_shapes=[
-            pltpu.VMEM((slab_count, rows, width), jnp.bfloat16),
-            dma((slab_count,)),
-        ],
-    )(slab_blocks, *tables, amplitudes)
     return pl.pallas_call(
         functools.partial(kernel, sizes),
         out_shape=jax.ShapeDtypeStruct((rows, columns), jnp.bfloat16),
-        in_specs=[smem, smem, vmem, hbm],
+        in_specs=[smem] + [vmem] * 4 + [hbm, hbm],
         out_specs=vmem,
         scratch_shapes=[
+            pltpu.VMEM((rows, columns), jnp.bfloat16),
+            pltpu.VMEM((span, rows, width), jnp.bfloat16),
+            pltpu.VMEM((slab_count, rows, width), jnp.bfloat16),
+            pltpu.VMEM((blks, width), jnp.int32),
+            pltpu.VMEM((16, span), jnp.int32),
+            pltpu.SMEM((blks, width), jnp.int32),
+            pltpu.SMEM((16, span), jnp.int32),
             pltpu.VMEM((slots, inner, width), jnp.bfloat16),
             pltpu.VMEM((blks, chunk, rows, width), jnp.bfloat16),
             pltpu.VMEM((pairs, blks, chunk, rows, width), jnp.bfloat16),
@@ -522,15 +523,15 @@
             dma((HALVES + 1, blks, pairs)),
             dma((HALVES + 1, blks)),
             dma((HALVES + 1, blks)),
-            dma((3,)),
+            dma((6,)),
         ],
         compiler_params=pltpu.CompilerParams(
             collective_id=0, has_side_effects=True, vmem_limit_bytes=56 * 2**20
         ),
     )(
-        slot_irrep,
-        meta,
-        picked,
+        slab_blocks,
+        *tables,
+        amplitudes,
         integrals.reshape(slots, inner, width),
     )
 

time: 117 us -> 114 us (0.974)
  Pallas kernels: 114 us -> 111 us
    pallas_call x1 -> x0, Pallas kernels: 3.67 us -> none  [local(): pl.pallas_call(functools.partial(prep_kernel, sizes), out_shape=(jax.Shap...]
where the time goes in v2:
time: 114 us
  Pallas kernels  111 us (97%)
  local copies, waits for them, and re-layouts  2.26 us (2%)
    pallas_call x1, Pallas kernels, local(): pl.pallas_call(functools.partial(kernel, sizes), out_shape=jax.ShapeDtype...  111 us

profile of v2, /device:TPU:13, one launch (start us, length us, event | category | flops | bytes accessed | tf_op | source)
XLA Modules:
  0.0 113.5 jit_solution(1472226712173310152)
XLA Ops:
  0.0 111.3 %shard_map.73 = bf16[16,32768]{1,0:T(8,128)(2,1)} custom-call(s32[32]{0:T(128)} %slab_ref.1, s32[16,128]{1,0:T(8,128)} %bitcast.6, s32[16,128]{1,0:T(8,128)} %bitcast.7, s32[16,128]{1,0:T(8,128)} %bitcast.8, s32[16,128]{1,0:T(8,128)} %bitcast.9, bf16[16,32768]{1,0:T(8,128)(2,1)} %amp_hbm.1, bf16[160,512,128]{2,1,0:T(8,128)(2,1)} %bitcast.5), custom_call_target="tpu_custom_call" | custom-call | tf_op jit(solution)/shard_map/pallas_call | solution.py:488
  111.3 2.3 %copy.9 = bf16[16,32768]{1,0:T(8,128)(2,1)} copy(bf16[16,32768]{1,0:T(8,128)(2,1)} %shard_map.73) | data formatting | bytes 2097152

commit v3 on v2

--- a/solution.py
+++ b/solution.py
@@ -128,6 +128,7 @@
     scale2,
     scale2_in,
     scale2_in_s,
+    factor_s,
     ints_sem,
     pick_send,
     pick_recv,
@@ -265,36 +266,33 @@
         for turn in range(pairs - 1):
             fwd_copy(blk_at(step), step, turn).start()
 
-    @pl.loop(0, blks - 1)
-    def _(step):
-        gath_copy(step).wait_send()
-
-    @pl.loop(0, blks)
-    def _(step):
-        for turn in range(pairs - 1):
-            fwd_copy(blk_at(step), step, turn).wait()
-
-    for n in range(slab_count):
-        for p in range(pairs):
-            slab[
-                n // per_irrep,
-                p * rows : (p + 1) * rows,
-                (n % per_irrep) * width : (n % per_irrep + 1) * width,
-            ] = slab_in[p, n // chunk, n % chunk]
-
     table_copy(irrep_v, irrep_ref, 1).wait()
     table_copy(meta_v, meta_ref, 2).wait()
 
-    def products(to):
+    def pair_at(turn):
+        return lax.rem(me_pair + turn, pairs)
+
+    def fill_slab(turns):
+        for n in range(slab_count):
+            columns = slice((n % per_irrep) * width, (n % per_irrep + 1) * width)
+            for turn in turns:
+                place = slice(turn * rows, (turn + 1) * rows)
+                slab[n // per_irrep, place, columns] = slab_in[pair_at(turn), n // chunk, n % chunk]
+
+    def products(to, turns):
+        low, high = turns[0] * rows, (turns[-1] + 1) * rows
+
         def slots(j, scales):
             coded = []
             for turn in range(2):
                 r = jnp.minimum(2 * j + turn, cap - 1)
                 product = jnp.dot(
-                    slab[jnp.clip(irrep_ref[to, r], 0, slab_count // per_irrep - 1)], ints[to * cap + r], preferred_element_type=jnp.float32
+                    slab[jnp.clip(irrep_ref[to, r], 0, slab_count // per_irrep - 1), low:high],
+                    ints[to * cap + r],
+                    preferred_element_type=jnp.float32,
                 )
                 tiles, found = [], []
-                for p in range(pairs):
+                for p in range(len(turns)):
                     tile = product[p * rows : (p + 1) * rows]
                     largest = jnp.max(jnp.abs(tile), axis=0, keepdims=True)
                     largest = jnp.maximum(jnp.max(largest, axis=1, keepdims=True), TINY)
@@ -302,16 +300,16 @@
                     found.append(jnp.where(lane == r, largest * (1.0 / TOP), scales[p]))
                 scales = tuple(found)
                 coded.append(tiles)
-            for p in range(pairs):
+            for p in range(len(turns)):
                 word = (coded[0][p] & 0xFFFF) | (coded[1][p] << 16)
                 for h in range(HALVES):
-                    send1[h][(to * pairs + p) * capw + j] = word[h * half : (h + 1) * half]
+                    send1[h][(to * pairs + pair_at(turns[p])) * capw + j] = word[h * half : (h + 1) * half]
             return scales
 
-        start = tuple(jnp.zeros((1, width), jnp.float32) for _ in range(pairs))
+        start = tuple(jnp.zeros((1, width), jnp.float32) for _ in turns)
         scales = lax.fori_loop(0, capw, slots, start, unroll=unroll_of(capw, 5))
-        for p in range(pairs):
-            scale1[to * pairs + p] = scales[p]
+        for p in range(len(turns)):
+            scale1[to * pairs + pair_at(turns[p])] = scales[p]
 
     def product_copy(h, step, turn):
         to = blk_at(step)
@@ -340,7 +338,10 @@
         return pltpu.make_async_copy(source, target, send1_sem.at[h, blks - 1, 0])
 
     def send_products(h):
-        @pl.loop(0, blks - 1)
+        for turn in range(1, pairs):
+            product_copy(h, 0, turn).start()
+
+        @pl.loop(1, blks - 1)
         def _(step):
             for turn in range(pairs):
                 product_copy(h, step, turn).start()
@@ -360,16 +361,38 @@
         for turn in range(1, pairs):
             product_copy(h, blks - 1, turn).wait()
 
+    ints_copy(0).wait()
+    fill_slab([0])
+    products(blk_at(0), [0])
+    for h in (HALVES, 0, 1):
+        product_copy(h, 0, 0).start()
+
     @pl.loop(0, blks - 1)
     def _(step):
+        gath_copy(step).wait_send()
+
+    @pl.loop(0, blks)
+    def _(step):
+        for turn in range(pairs - 1):
+            fwd_copy(blk_at(step), step, turn).wait()
+
+    every_turn = list(range(pairs))
+    fill_slab(every_turn[1:])
+    products(blk_at(0), every_turn[1:])
+    for h in (HALVES, 0):
+        for turn in range(1, pairs):
+            product_copy(h, 0, turn).start()
+
+    @pl.loop(1, blks - 1)
+    def _(step):
         ints_copy(step).wait()
-        products(blk_at(step))
+        products(blk_at(step), every_turn)
         for h in (HALVES, 0):
             for turn in range(pairs):
                 product_copy(h, step, turn).start()
 
     ints_copy(blks - 1).wait()
-    products(me_blk)
+    products(me_blk, every_turn)
     for h in (HALVES, 0):
         keep_copy(h).start()
         for turn in range(1, pairs):
@@ -419,7 +442,12 @@
 
     def finish(h):
         def out_entry(i, carry):
-            scale = scale2_in_s[jnp.clip(meta_ref[8, i], 0, blks - 1), 0, jnp.clip(meta_ref[9, i], 0, width - 1)] * meta_ref[12, i].astype(jnp.float32)
+            if h == 0:
+                place = (jnp.clip(meta_ref[8, i], 0, blks - 1), jnp.clip(meta_ref[9, i], 0, width - 1))
+                scale = scale2_in_s[place[0], 0, place[1]] * meta_ref[12, i].astype(jnp.float32)
+                factor_s[i] = scale
+            else:
+                scale = factor_s[i]
             mirrored = value_of(recv2[h][jnp.clip(meta_ref[10, i], 0, span // 2 - 1)], meta_ref[11, i])
             total = own[h, i] + mirrored * scale
             columns = pl.ds(pl.multiple_of(i * width, width), width)
@@ -512,6 +540,7 @@
             pltpu.VMEM((blks, 1, width), jnp.float32),
             pltpu.VMEM((blks, 1, width), jnp.float32),
             pltpu.SMEM((blks, 1, width), jnp.float32),
+            pltpu.SMEM((span,), jnp.float32),
             dma((blks,)),
             dma((blks,)),
             dma((blks,)),

time: 114 us -> 110 us (0.965)
  Pallas kernels: 111 us -> 107 us
    pallas_call x1, Pallas kernels: 111 us -> 107 us  [local(): pl.pallas_call(functools.partial(kernel, sizes), out_shape=jax.ShapeDtype...]
where the time goes in v3:
time: 110 us; the launch traced here: 109 us
  Pallas kernels  107 us (97%)
  local copies, waits for them, and re-layouts  2.26 us (2%)
    pallas_call x1, Pallas kernels, local(): pl.pallas_call(functools.partial(kernel, sizes), out_shape=jax.ShapeDtype...  107 us
    unnamed x1, local copies, waits for them, and re-layouts  2.26 us

profile of v3, /device:TPU:13, one launch (start us, length us, event | category | flops | bytes accessed | tf_op | source)
XLA Modules:
  0.0 109.2 jit_solution(13890611169057432596)
XLA Ops:
  0.0 106.9 %shard_map.73 = bf16[16,32768]{1,0:T(8,128)(2,1)} custom-call(s32[32]{0:T(128)} %slab_ref.1, s32[16,128]{1,0:T(8,128)} %bitcast.6, s32[16,128]{1,0:T(8,128)} %bitcast.7, s32[16,128]{1,0:T(8,128)} %bitcast.8, s32[16,128]{1,0:T(8,128)} %bitcast.9, bf16[16,32768]{1,0:T(8,128)(2,1)} %amp_hbm.1, bf16[160,512,128]{2,1,0:T(8,128)(2,1)} %bitcast.5), custom_call_target="tpu_custom_call" | custom-call | tf_op jit(solution)/shard_map/pallas_call | solution.py:516
  106.9 2.3 %copy.9 = bf16[16,32768]{1,0:T(8,128)(2,1)} copy(bf16[16,32768]{1,0:T(8,128)(2,1)} %shard_map.73) | data formatting | bytes 2097152

commit v4 on v3

--- a/solution.py
+++ b/solution.py
@@ -179,14 +179,13 @@
 
     barrier = pltpu.get_barrier_semaphore()
 
-    @pl.loop(1, devices)
-    def _(step):
-        other = lax.rem(me + step, devices)
+    @pl.loop(0, blks - 1)
+    def _(step):
+        pl.semaphore_signal(barrier, inc=1, device_id={"blk": blk_at(step)}, device_id_type=MESH)
+
+    for turn in range(1, pairs):
         pl.semaphore_signal(
-            barrier,
-            inc=1,
-            device_id={"blk": other // pairs, "pair": lax.rem(other, pairs)},
-            device_id_type=MESH,
+            barrier, inc=1, device_id={"pair": lax.rem(me_pair + turn, pairs)}, device_id_type=MESH
         )
 
     table_copy(amp_hbm, amp, 0).wait()
@@ -202,7 +201,7 @@
         block = amp_blocks[jnp.clip(local, 0, span - 1)]
         picked[n] = (block.astype(jnp.float32) * inside).astype(jnp.bfloat16)
 
-    pl.semaphore_wait(barrier, devices - 1)
+    pl.semaphore_wait(barrier, blks + pairs - 2)
 
     def pick_copy(step):
         to = blk_at(step)

time: 110 us -> 108 us (0.982)
  Pallas kernels: 107 us -> 104 us
    pallas_call x1, Pallas kernels: 107 us -> 104 us  [local(): pl.pallas_call(functools.partial(kernel, sizes), out_shape=jax.ShapeDtype...]
where the time goes in v4:
time: 108 us; the launch traced here: 107 us
  Pallas kernels  104 us (96%)
  local copies, waits for them, and re-layouts  2.26 us (2%)
    pallas_call x1, Pallas kernels, local(): pl.pallas_call(functools.partial(kernel, sizes), out_shape=jax.ShapeDtype...  104 us
    unnamed x1, local copies, waits for them, and re-layouts  2.26 us

profile of v4, /device:TPU:13, one launch (start us, length us, event | category | flops | bytes accessed | tf_op | source)
XLA Modules:
  0.0 106.6 jit_solution(11024659350611531051)
XLA Ops:
  0.0 104.3 %shard_map.73 = bf16[16,32768]{1,0:T(8,128)(2,1)} custom-call(s32[32]{0:T(128)} %slab_ref.1, s32[16,128]{1,0:T(8,128)} %bitcast.6, s32[16,128]{1,0:T(8,128)} %bitcast.7, s32[16,128]{1,0:T(8,128)} %bitcast.8, s32[16,128]{1,0:T(8,128)} %bitcast.9, bf16[16,32768]{1,0:T(8,128)(2,1)} %amp_hbm.1, bf16[160,512,128]{2,1,0:T(8,128)(2,1)} %bitcast.5), custom_call_target="tpu_custom_call" | custom-call | tf_op jit(solution)/shard_map/pallas_call | solution.py:515
  104.3 2.3 %copy.9 = bf16[16,32768]{1,0:T(8,128)(2,1)} copy(bf16[16,32768]{1,0:T(8,128)(2,1)} %shard_map.73) | data formatting | bytes 2097152

commit v5 on v4

--- a/solution.py
+++ b/solution.py
@@ -93,14 +93,19 @@
 
 def kernel(
     sizes,
+    slab_hbm,
+    owner_hbm,
+    partner_hbm,
+    irreps_hbm,
+    sign_hbm,
+    amp_hbm,
+    ints_hbm,
+    out_ref,
     slab_ref,
     owner_ref,
     partner_ref,
     irreps_ref,
     sign_ref,
-    amp_hbm,
-    ints_hbm,
-    out_ref,
     amp,
     amp_blocks,
     picked,
@@ -141,6 +146,9 @@
     send2_sem,
     recv2_sem,
     table_sem,
+    out_a,
+    out_b,
+    out_sem,
 ):
     blks, pairs, span, cap, per_irrep, slab_count, rows, width = sizes
     devices = blks * pairs
@@ -153,6 +161,7 @@
     lane = lax.broadcasted_iota(jnp.int32, (1, width), 1)
     send1, recv1 = (send1a, send1b), (recv1a, recv1b)
     send2, recv2 = (send2a, send2b), (recv2a, recv2b)
+    out_v = (out_a, out_b)
 
     def blk_at(step):
         pattern = blks // 2 + (1 - step % 2) * (step // 2) - (step % 2) * ((step + 1) // 2)
@@ -171,11 +180,21 @@
     def table_copy(source, target, at):
         return pltpu.make_async_copy(source, target, table_sem.at[at])
 
+    entry_copies = [
+        table_copy(source, target, 6 + at)
+        for at, (source, target) in enumerate(
+            (
+                (slab_hbm, slab_ref),
+                (owner_hbm, owner_ref),
+                (partner_hbm, partner_ref),
+                (irreps_hbm, irreps_ref),
+                (sign_hbm, sign_ref),
+            )
+        )
+    ]
     table_copy(amp_hbm, amp, 0).start()
-
-    @pl.loop(0, blks)
-    def _(step):
-        ints_copy(step).start()
+    for copy in entry_copies:
+        copy.start()
 
     barrier = pltpu.get_barrier_semaphore()
 
@@ -188,6 +207,10 @@
             barrier, inc=1, device_id={"pair": lax.rem(me_pair + turn, pairs)}, device_id_type=MESH
         )
 
+    @pl.loop(0, blks)
+    def _(step):
+        ints_copy(step).start()
+
     table_copy(amp_hbm, amp, 0).wait()
 
     def split(i, carry):
@@ -195,6 +218,7 @@
         return carry
 
     lax.fori_loop(0, span, split, 0, unroll=unroll_of(span, 8))
+    entry_copies[0].wait()
     for n in range(slab_count):
         local = slab_ref[n] - me_blk * span
         inside = jnp.logical_and(local >= 0, local < span).astype(jnp.float32)
@@ -218,6 +242,8 @@
     def _(step):
         pick_copy(step).start()
 
+    for copy in entry_copies[1:]:
+        copy.wait()
     fill_tables(sizes, owner_ref, partner_ref, irreps_ref, sign_ref, irrep_v, meta_v)
     table_copy(irrep_v, irrep_ref, 1).start()
     table_copy(meta_v, meta_ref, 2).start()
@@ -450,10 +476,22 @@
             mirrored = value_of(recv2[h][jnp.clip(meta_ref[10, i], 0, span // 2 - 1)], meta_ref[11, i])
             total = own[h, i] + mirrored * scale
             columns = pl.ds(pl.multiple_of(i * width, width), width)
-            out_ref[h * half : (h + 1) * half, columns] = total.astype(jnp.bfloat16)
+            out_v[h][:, columns] = total.astype(jnp.bfloat16)
             return carry
 
-        lax.fori_loop(0, span, out_entry, 0, unroll=unroll_of(span, 8))
+        copies = []
+        for part in range(4):
+            low, high = part * span // 4, (part + 1) * span // 4
+            lax.fori_loop(low, high, out_entry, 0, unroll=unroll_of(high - low, 8))
+            columns = slice(low * width, high * width)
+            copy = pltpu.make_async_copy(
+                out_v[h].at[:, columns],
+                out_ref.at[h * half : (h + 1) * half, columns],
+                out_sem.at[h, part],
+            )
+            copy.start()
+            copies.append(copy)
+        return copies
 
     wait_products(HALVES)
     table_copy(scale1_in, scale1_s, 3).start()
@@ -482,13 +520,16 @@
     table_copy(scale2_in, scale2_in_s, 5).wait()
     wait_products(1)
     gather(1)
+    outs = []
     for h in range(HALVES):
 
         @pl.loop(0, blks)
         def _(step):
             mirror_copy(h, step).wait()
 
-        finish(h)
+        outs += finish(h)
+    for copy in outs:
+        copy.wait()
 
 
 def local(amplitudes, integrals, block_irrep, slab_blocks, owner, partner, sign):
@@ -508,16 +549,16 @@
     tables = [table.reshape(-1, width) for table in (owner, partner, block_irrep, sign)]
 
     sizes = (blks, pairs, span, cap, per_irrep, slab_count, rows, width)
-    smem = pl.BlockSpec(memory_space=pltpu.SMEM)
-    vmem = pl.BlockSpec(memory_space=pltpu.VMEM)
     dma = pltpu.SemaphoreType.DMA
     hbm = pl.BlockSpec(memory_space=pl.ANY)
     return pl.pallas_call(
         functools.partial(kernel, sizes),
         out_shape=jax.ShapeDtypeStruct((rows, columns), jnp.bfloat16),
-        in_specs=[smem] + [vmem] * 4 + [hbm, hbm],
-        out_specs=vmem,
+        in_specs=[hbm] * 7,
+        out_specs=hbm,
         scratch_shapes=[
+            pltpu.SMEM(slab_blocks.shape, jnp.int32),
+            *[pltpu.VMEM(table.shape, jnp.int32) for table in tables],
             pltpu.VMEM((rows, columns), jnp.bfloat16),
             pltpu.VMEM((span, rows, width), jnp.bfloat16),
             pltpu.VMEM((slab_count, rows, width), jnp.bfloat16),
@@ -551,7 +592,9 @@
             dma((HALVES + 1, blks, pairs)),
             dma((HALVES + 1, blks)),
             dma((HALVES + 1, blks)),
-            dma((6,)),
+            dma((11,)),
+            *[pltpu.VMEM((half, columns), jnp.bfloat16)] * HALVES,
+            dma((HALVES, 4)),
         ],
         compiler_params=pltpu.CompilerParams(
             collective_id=0, has_side_effects=True, vmem_limit_bytes=56 * 2**20

time: 108 us -> 107 us (level)
    pallas_call x1, Pallas kernels: 104 us -> 103 us  [local(): pl.pallas_call(functools.partial(kernel, sizes), out_shape=jax.ShapeDtype...]
where the time goes in v5:
time: 107 us; the launch traced here: 105 us
  Pallas kernels  103 us (96%)
  local copies, waits for them, and re-layouts  2.26 us (2%)
    pallas_call x1, Pallas kernels, local(): pl.pallas_call(functools.partial(kernel, sizes), out_shape=jax.ShapeDtype...  103 us
    unnamed x1, local copies, waits for them, and re-layouts  2.26 us

profile of v5, /device:TPU:13, one launch (start us, length us, event | category | flops | bytes accessed | tf_op | source)
XLA Modules:
  0.0 105.3 jit_solution(5870838350566435622)
XLA Ops:
  0.0 103.0 %shard_map.73 = bf16[16,32768]{1,0:T(8,128)(2,1)} custom-call(s32[32]{0:T(128)} %slab_hbm.1, s32[16,128]{1,0:T(8,128)} %bitcast.6, s32[16,128]{1,0:T(8,128)} %bitcast.7, s32[16,128]{1,0:T(8,128)} %bitcast.8, s32[16,128]{1,0:T(8,128)} %bitcast.9, bf16[16,32768]{1,0:T(8,128)(2,1)} %amp_hbm.1, bf16[160,512,128]{2,1,0:T(8,128)(2,1)} %bitcast.5), custom_call_target="tpu_custom_call" | custom-call | tf_op jit(solution)/shard_map/pallas_call | solution.py:554
  103.0 2.3 %copy.9 = bf16[16,32768]{1,0:T(8,128)(2,1)} copy(bf16[16,32768]{1,0:T(8,128)(2,1)} %shard_map.73) | data formatting | bytes 2097152
